TPU v7x, 256 devices: a whole 4x4x8 slice. The times are simulated.
256 devices in a mesh: depth: 4 (over x), row: 16 (over z, y_hi), col: 4 (over y_lo, core).
Axes of the slice: x: 4, y: 4 (y_hi: 2, y_lo: 2; y = y_hi * 2 + y_lo), z: 8, core: 2. Of those that a mesh axis runs over, the one named last changes fastest.
Arguments:
- tokens: bfloat16 [768, 8192], P(('depth', 'row')), may hold values from -6 to 6
- out_grad: bfloat16 [768, 8192], P(('depth', 'row')), may hold values from -0.59765625 to 0.59765625
- gate_weight: bfloat16 [8192, 16384], P('depth', ('row', 'col')), may hold values from -0.0625 to 0.0625
- up_weight: bfloat16 [8192, 16384], P('depth', ('row', 'col')), may hold values from -0.0625 to 0.0625
- down_weight: bfloat16 [16384, 8192], P(('row', 'col'), 'depth'), may hold values from -0.046875 to 0.046875
Outputs:
- input_grad: bfloat16 [768, 8192], P(('depth', 'row', 'col'))
- gate_grad: bfloat16 [8192, 16384], P('depth', ('row', 'col'))
- up_grad: bfloat16 [8192, 16384], P('depth', ('row', 'col'))
- down_grad: bfloat16 [16384, 8192], P(('row', 'col'), 'depth')
All inputs are finite; a program needn't handle non-finite values.
Results may differ from a plain program's by a relative error of at most 0.024.
Values may be sent and summed in bfloat16 or wider, within the bound.
No kernel may reach another device: no remote copies, remote signals or barrier semaphores. Data moves between devices by JAX's collectives and lax.ppermute only.
A program may use at most 128 MiB of HBM per device.

v0:
```python
import jax
import jax.numpy as jnp
from jax import lax
from jax.sharding import PartitionSpec as P


def contract_rows(left, right):
    return lax.dot_general(
        left, right, (((0,), (0,)), ((), ())), preferred_element_type=jnp.float32
    )


def contract_cols(left, right):
    return lax.dot_general(
        left, right, (((1,), (1,)), ((), ())), preferred_element_type=jnp.float32
    )


def swiglu_terms(gate, up, hidden_grad):
    sig = jax.nn.sigmoid(gate)
    act = gate * sig
    hidden = (act * up).astype(jnp.bfloat16)
    gate_term = (hidden_grad * up * sig * (1.0 + gate * (1.0 - sig))).astype(jnp.bfloat16)
    up_term = (hidden_grad * act).astype(jnp.bfloat16)
    return (hidden, gate_term, up_term)


def block_work(tok_part, grad_part, gate_full, up_full, down_full):
    gate = jnp.dot(tok_part, gate_full, preferred_element_type=jnp.float32)
    up = jnp.dot(tok_part, up_full, preferred_element_type=jnp.float32)
    hidden_grad = contract_cols(grad_part, down_full)
    hidden, gate_term, up_term = swiglu_terms(gate, up, hidden_grad)
    partial_in = contract_cols(gate_term, gate_full) + contract_cols(up_term, up_full)
    return (hidden, gate_term, up_term, partial_in)


def on_device(tokens, out_grad, gate_weight, up_weight, down_weight):
    gate_full, up_full, down_full = (
        lax.all_gather(gate_weight, "depth", axis=0, tiled=True),
        lax.all_gather(up_weight, "depth", axis=0, tiled=True),
        lax.all_gather(down_weight, "depth", axis=1, tiled=True),
    )
    all_tok, all_grad = (
        lax.all_gather(tokens, "row", axis=0, tiled=True),
        lax.all_gather(out_grad, "row", axis=0, tiled=True),
    )
    hidden, gate_term, up_term, partial_in = block_work(
        all_tok, all_grad, gate_full, up_full, down_full
    )
    input_grad = lax.psum_scatter(
        partial_in, ("row", "col"), scatter_dimension=0, tiled=True
    ).astype(jnp.bfloat16)
    gate_grad, up_grad, down_grad = (
        lax.psum_scatter(
            contract_rows(all_tok, gate_term).astype(jnp.bfloat16),
            "depth",
            scatter_dimension=0,
            tiled=True,
        ).astype(jnp.float32),
        lax.psum_scatter(
            contract_rows(all_tok, up_term).astype(jnp.bfloat16),
            "depth",
            scatter_dimension=0,
            tiled=True,
        ).astype(jnp.float32),
        lax.psum_scatter(
            contract_rows(hidden, all_grad).astype(jnp.bfloat16),
            "depth",
            scatter_dimension=1,
            tiled=True,
        ).astype(jnp.float32),
    )
    return (
        input_grad,
        gate_grad.astype(jnp.bfloat16),
        up_grad.astype(jnp.bfloat16),
        down_grad.astype(jnp.bfloat16),
    )


def solution(mesh):
    return jax.shard_map(
        on_device,
        mesh=mesh,
        in_specs=(
            P(("depth", "row"), None),
            P(("depth", "row"), None),
            P("depth", ("row", "col")),
            P("depth", ("row", "col")),
            P(("row", "col"), "depth"),
        ),
        out_specs=(
            P(("depth", "row", "col"), None),
            P("depth", ("row", "col")),
            P("depth", ("row", "col")),
            P(("row", "col"), "depth"),
        ),
        check_vma=False,
    )
```

profile of v0, /device:TPU:2, one launch (start us, length us, event | category | flops | bytes accessed | tf_op | source)
XLA Modules:
  0.0 703.7 jit_solution(15544658315042769333)
XLA Ops:
  7.2 0.0 all-gather.16.cloned.1.call-start
  7.2 0.7 all-gather.16.cloned.1.call-update
  7.9 0.0 all-gather.14.cloned.1.call-start
  7.9 0.7 all-gather.14.cloned.1.call-update
  8.6 0.0 all-gather.10.cloned.1.call-start
  8.7 0.7 all-gather.10.cloned.1.call-update
  9.4 0.0 all-gather.12.cloned.1.call-start
  9.4 0.5 all-gather.12.cloned.1.call-update
  10.0 0.0 all-gather.8.cloned.1.call-start
  10.0 0.5 all-gather.8.cloned.1.call-update
  10.5 0.0 reduce-scatter.6.cloned.1.call-start
  10.6 103.0 %all-gather.16.cloned.1.call-done = bf16[16,12,8192]{2,1,0:T(8,128)(2,1)} async-done(((bf16[1,12,8192]{2,1,0:T(8,128)(2,1)}), bf16[16,12,8192]{2,1,0:T(8,128)(2,1)}) %all-gather.16.cloned.1.call-update) | async-done | bytes 3145744 | tf_op jit(solution)/shard_map/all_gather | solution.py:44
  113.6 3.2 reshape.11
  116.9 95.9 %all-gather.14.cloned.1.call-done = bf16[16,12,8192]{2,1,0:T(8,128)(2,1)} async-done(((bf16[1,12,8192]{2,1,0:T(8,128)(2,1)}), bf16[16,12,8192]{2,1,0:T(8,128)(2,1)}) %all-gather.14.cloned.1.call-update) | async-done | bytes 3145744 | tf_op jit(solution)/shard_map/all_gather | solution.py:45
  212.7 4.7 reshape.9
  217.4 43.8 %all-gather.10.cloned.1.call-done = bf16[8192,256]{1,0:T(8,128)(2,1)} async-done(((bf16[2048,256]{1,0:T(8,128)(2,1)}), bf16[8192,256]{1,0:T(8,128)(2,1)}) %all-gather.10.cloned.1.call-update) | async-done | bytes 4194320 | tf_op jit(solution)/shard_map/all_gather | solution.py:40
  261.3 3.2 fusion.5
  264.4 49.7 %all-gather.12.cloned.1.call-done = bf16[8192,256]{1,0:T(8,128)(2,1)} async-done(((bf16[2048,256]{1,0:T(8,128)(2,1)}), bf16[8192,256]{1,0:T(8,128)(2,1)}) %all-gather.12.cloned.1.call-update) | async-done | bytes 4194320 | tf_op jit(solution)/shard_map/all_gather | solution.py:39
  314.1 3.2 fusion.6
  317.3 49.7 %all-gather.8.cloned.1.call-done = bf16[256,8192]{1,0:T(8,128)(2,1)} async-done(((bf16[256,2048]{1,0:T(8,128)(2,1)}), bf16[256,8192]{1,0:T(8,128)(2,1)}) %all-gather.8.cloned.1.call-update) | async-done | bytes 4194320 | tf_op jit(solution)/shard_map/all_gather | solution.py:41
  367.0 5.3 multiply_convert_fusion.1
  372.3 0.0 copy-start.3
  372.3 0.6 copy-done.3
  373.0 3.2 fusion.1
  376.2 0.0 reduce-scatter.6.cloned.1.call-update
  376.2 0.0 reduce-scatter.4.cloned.1.call-start
  376.2 4.2 fusion
  380.4 0.0 copy-start.1
  380.4 0.0 reduce-scatter.4.cloned.1.call-update
  380.4 0.0 copy-start.5
  380.4 0.0 reduce-scatter.8.cloned.1.call-start
  380.5 1.8 copy-done.1
  382.3 3.3 convolution_convert_fusion
  385.5 0.0 copy-start.2
  385.5 0.0 reduce-scatter.8.cloned.1.call-update
  385.6 0.0 copy-done.5
  385.6 0.6 dynamic-slice
  386.8 0.0 copy-done.2
  386.8 0.0 copy-start
  386.8 0.0 copy-start.4
  386.8 4.4 fusion.7
  391.2 0.0 copy-done
  391.2 0.0 copy-done.4
  391.2 4.2 convolution_add_fusion
  395.4 296.2 %all-reduce.2 = bf16[192,8192]{1,0:T(8,128)(2,1)S(1)} all-reduce(f32[192,8192]{1,0:T(8,128)} %convolution_add_fusion), channel_id=2, replica_groups=mesh['depth'=4,'row'=16,'col'=4] {'row','col'}, use_global_device_ids=true, to_apply=%region_0.0.clone | all-reduce | flops 1572864 | bytes 9437184
  691.6 0.7 dynamic-slice_convert_fusion
  692.3 0.0 reduce-scatter.6.cloned.1.call-done
  692.3 2.3 copy.14
  694.6 0.0 reduce-scatter.4.cloned.1.call-done
  694.6 2.3 copy.13
  696.8 0.0 reduce-scatter.8.cloned.1.call-done
Async XLA Ops:
  7.2 106.4 %all-gather.16.cloned.1.call-start = ((), (), s32[]{:S(2)}) async-start(), calls=%async_computation.10 | async-start | bytes 4456448 | tf_op jit(solution)/shard_map/all_gather | solution.py:44
  7.9 204.8 %all-gather.14.cloned.1.call-start = ((), (), s32[]{:S(2)}) async-start(), calls=%async_computation.9 | async-start | bytes 4456448 | tf_op jit(solution)/shard_map/all_gather | solution.py:45
  8.6 252.6 %all-gather.10.cloned.1.call-start = ((), (), s32[]{:S(2)}) async-start(), calls=%async_computation.4 | async-start | bytes 5242880 | tf_op jit(solution)/shard_map/all_gather | solution.py:40
  9.4 304.7 %all-gather.12.cloned.1.call-start = ((), (), s32[]{:S(2)}) async-start(), calls=%async_computation.5 | async-start | bytes 5242880 | tf_op jit(solution)/shard_map/all_gather | solution.py:39
  10.0 357.0 %all-gather.8.cloned.1.call-start = ((), (), s32[]{:S(2)}) async-start(), calls=%async_computation.3 | async-start | bytes 5242880 | tf_op jit(solution)/shard_map/all_gather | solution.py:41
  10.5 681.7 %reduce-scatter.6.cloned.1.call-start = ((), (), s32[]{:S(2)}) async-start(), calls=%async_computation.7 | async-start | bytes 5242880 | tf_op jit(solution)/shard_map/reduce_scatter | solution.py:60
  372.3 0.6 copy-start.3
  376.2 318.4 %reduce-scatter.4.cloned.1.call-start = ((), (), s32[]{:S(2)}) async-start(), calls=%async_computation.6 | async-start | bytes 5242880 | tf_op jit(solution)/shard_map/reduce_scatter | solution.py:54
  380.4 1.9 copy-start.1
  380.4 5.1 copy-start.5
  380.4 316.4 %reduce-scatter.8.cloned.1.call-start = ((), (), s32[]{:S(2)}) async-start(), calls=%async_computation.8 | async-start | bytes 5242880 | tf_op jit(solution)/shard_map/reduce_scatter | solution.py:66
  385.5 1.3 copy-start.2
  386.8 4.4 copy-start
  386.8 4.4 copy-start.4
Sparse Core Ops, SparseCore 0:
  10.6 102.9 all-gather.15
  116.2 96.5 all-gather.13
  214.6 46.6 all-gather.9
  262.9 51.1 all-gather.11
  315.8 51.1 all-gather.7
  376.3 49.0 reduce-scatter.5
  428.2 49.0 reduce-scatter.3
  480.4 49.0 reduce-scatter.7
where the time goes:
time: 704 us
  waiting for transfers between devices  345 us (49%)
  blocking collectives  296 us (42%)
  matrix products  30.8 us (4%)
  local copies, waits for them, and re-layouts  16.2 us (2%)
  between operations  14.9 us (2%)
    unnamed x1, blocking collectives  296 us
    all_gather x1, waiting for transfers between devices, on_device(): lax.all_gather(tokens, 'row', axis=0, tiled=True)  103 us
    all_gather x1, waiting for transfers between devices, on_device(): lax.all_gather(out_grad, 'row', axis=0, tiled=True)  95.9 us
    all_gather x1, waiting for transfers between devices, on_device(): lax.all_gather(gate_weight, 'depth', axis=0, tiled=True)  49.7 us
    all_gather x1, waiting for transfers between devices, on_device(): lax.all_gather(down_weight, 'depth', axis=1, tiled=True)  49.7 us
    all_gather x1, waiting for transfers between devices, on_device(): lax.all_gather(up_weight, 'depth', axis=0, tiled=True)  43.8 us
    unnamed x17, local copies, waits for them, and re-layouts  15.5 us
  transfers between devices with their start and end apart: 8, of which 5 were waited for; matrix products, arithmetic and copies ran while one was open for 5% of the time, Pallas kernels for 0%

commit v1 on v0

--- a/solution.py
+++ b/solution.py
@@ -36,7 +36,9 @@
 
 def on_device(tokens, out_grad, gate_weight, up_weight, down_weight):
     gate_full, up_full, down_full = (
-        lax.all_gather(gate_weight, "depth", axis=0, tiled=True),
+        jnp.concatenate(
+            lax.all_to_all(jnp.stack([gate_weight] * lax.axis_size("depth")), "depth", 0, 0), axis=0
+        ),
         lax.all_gather(up_weight, "depth", axis=0, tiled=True),
         lax.all_gather(down_weight, "depth", axis=1, tiled=True),
     )

time: 704 us -> 651 us (0.925)
  waiting for transfers between devices: 345 us -> 282 us
    all_gather x1 -> x0, waiting for transfers between devices: 49.7 us -> none  [on_device(): lax.all_gather(gate_weight, 'depth', axis=0, tiled=True)]
    all_gather x1, waiting for transfers between devices: 103 us -> 93.1 us  [on_device(): lax.all_gather(tokens, 'row', axis=0, tiled=True)]
    all_to_all x0 -> x1, starting transfers between devices: none -> 7.07 us  [on_device(): lax.all_to_all(jnp.stack([gate_weight] * lax.axis_size('depth')), 'depth'...]
  transfers between devices with their start and end apart: 8 -> 8, of which waited for: 5 -> 4; matrix products, arithmetic and copies ran while one was open for 5% -> 6% of each run, Pallas kernels for 0% -> 0%
where the time goes in v1:
time: 651 us
  blocking collectives  296 us (45%)
  waiting for transfers between devices  282 us (43%)
  matrix products  30.8 us (5%)
  local copies, waits for them, and re-layouts  19.7 us (3%)
  between operations  14.9 us (2%)
  starting transfers between devices  7.31 us (1%)
    unnamed x1, blocking collectives  296 us
    all_gather x1, waiting for transfers between devices, on_device(): lax.all_gather(out_grad, 'row', axis=0, tiled=True)  95.9 us
    all_gather x1, waiting for transfers between devices, on_device(): lax.all_gather(tokens, 'row', axis=0, tiled=True)  93.1 us
    all_gather x1, waiting for transfers between devices, on_device(): lax.all_gather(down_weight, 'depth', axis=1, tiled=True)  49.7 us
    all_gather x1, waiting for transfers between devices, on_device(): lax.all_gather(up_weight, 'depth', axis=0, tiled=True)  40.6 us
    unnamed x17, local copies, waits for them, and re-layouts  15.5 us
    dot_general x3, matrix products, contract_cols(): lax.dot_general(left, right, (((1,), (1,)), ((), ())), preferred_element_...  13.8 us
  transfers between devices with their start and end apart: 8, of which 4 were waited for; matrix products, arithmetic and copies ran while one was open for 6% of the time, Pallas kernels for 0%

profile of v1, /device:TPU:2, one launch (start us, length us, event | category | flops | bytes accessed | tf_op | source)
XLA Modules:
  0.0 650.8 jit_solution(3058405788610709587)
XLA Ops:
  7.2 0.0 all-gather.13.cloned.1.call-start
  7.2 0.7 all-gather.13.cloned.1.call-update
  7.9 0.0 all-gather.11.cloned.1.call-start
  7.9 0.7 all-gather.11.cloned.1.call-update
  8.6 0.0 all-gather.9.cloned.1.call-start
  8.7 0.7 all-gather.9.cloned.1.call-update
  9.4 0.0 all-gather.7.cloned.1.call-start
  9.4 0.5 all-gather.7.cloned.1.call-update
  10.0 3.5 stack.2
  13.4 7.1 %all-to-all-start = ((bf16[4,2048,256]{2,1,0:T(8,128)(2,1)}), bf16[4,2048,256]{2,1,0:T(8,128)(2,1)}, u32[]{:S(2)}, u32[]{:S(2)}) async-start(bf16[4,2048,256]{2,1,0:T(8,128)(2,1)} %stack.2), calls=%async_computation | async-start | bytes 8388608 | tf_op jit(solution)/shard_map/all_to_all | solution.py:40
  20.5 0.0 reduce-scatter.4.cloned.1.call-start
  20.5 93.1 %all-gather.13.cloned.1.call-done = bf16[16,12,8192]{2,1,0:T(8,128)(2,1)} async-done(((bf16[1,12,8192]{2,1,0:T(8,128)(2,1)}), bf16[16,12,8192]{2,1,0:T(8,128)(2,1)}) %all-gather.13.cloned.1.call-update) | async-done | bytes 3145744 | tf_op jit(solution)/shard_map/all_gather | solution.py:46
  113.6 3.2 reshape.17
  116.9 95.9 %all-gather.11.cloned.1.call-done = bf16[16,12,8192]{2,1,0:T(8,128)(2,1)} async-done(((bf16[1,12,8192]{2,1,0:T(8,128)(2,1)}), bf16[16,12,8192]{2,1,0:T(8,128)(2,1)}) %all-gather.11.cloned.1.call-update) | async-done | bytes 3145744 | tf_op jit(solution)/shard_map/all_gather | solution.py:47
  212.7 4.7 reshape.15
  217.4 0.0 all-to-all-done
  217.4 3.2 fusion.6
  220.6 40.6 %all-gather.9.cloned.1.call-done = bf16[8192,256]{1,0:T(8,128)(2,1)} async-done(((bf16[2048,256]{1,0:T(8,128)(2,1)}), bf16[8192,256]{1,0:T(8,128)(2,1)}) %all-gather.9.cloned.1.call-update) | async-done | bytes 4194320 | tf_op jit(solution)/shard_map/all_gather | solution.py:42
  261.3 3.2 fusion.5
  264.4 49.7 %all-gather.7.cloned.1.call-done = bf16[256,8192]{1,0:T(8,128)(2,1)} async-done(((bf16[256,2048]{1,0:T(8,128)(2,1)}), bf16[256,8192]{1,0:T(8,128)(2,1)}) %all-gather.7.cloned.1.call-update) | async-done | bytes 4194320 | tf_op jit(solution)/shard_map/all_gather | solution.py:43
  314.1 5.3 multiply_convert_fusion.1
  319.5 0.0 copy-start.2
  319.5 0.6 copy-done.2
  320.1 3.2 fusion
  323.3 0.0 reduce-scatter.4.cloned.1.call-update
  323.4 0.0 reduce-scatter.6.cloned.1.call-start
  323.4 4.1 fusion.1
  327.5 0.0 copy-start.1
  327.5 0.0 reduce-scatter.6.cloned.1.call-update
  327.5 0.0 copy-start.5
  327.5 0.0 reduce-scatter.8.cloned.1.call-start
  327.6 1.8 copy-done.1
  329.4 3.3 convolution_convert_fusion
  332.7 0.0 copy-start.3
  332.7 0.0 reduce-scatter.8.cloned.1.call-update
  332.7 0.0 copy-done.5
  332.7 0.6 dynamic-slice
  333.9 0.0 copy-done.3
  333.9 0.0 copy-start
  334.0 0.0 copy-start.4
  334.0 4.3 fusion.7
  338.3 0.0 copy-done
  338.3 0.0 copy-done.4
  338.3 4.2 convolution_add_fusion
  342.5 296.2 %all-reduce.2 = bf16[192,8192]{1,0:T(8,128)(2,1)S(1)} all-reduce(f32[192,8192]{1,0:T(8,128)} %convolution_add_fusion), channel_id=2, replica_groups=mesh['depth'=4,'row'=16,'col'=4] {'row','col'}, use_global_device_ids=true, to_apply=%region_0.0.clone | all-reduce | flops 1572864 | bytes 9437184
  638.7 0.7 dynamic-slice_convert_fusion
  639.4 0.0 reduce-scatter.4.cloned.1.call-done
  639.4 2.3 copy.13
  641.7 0.0 reduce-scatter.6.cloned.1.call-done
  641.7 2.3 copy.14
  643.9 0.0 reduce-scatter.8.cloned.1.call-done
Async XLA Ops:
  7.2 106.4 %all-gather.13.cloned.1.call-start = ((), (), s32[]{:S(2)}) async-start(), calls=%async_computation.10 | async-start | bytes 4456448 | tf_op jit(solution)/shard_map/all_gather | solution.py:46
  7.9 204.8 %all-gather.11.cloned.1.call-start = ((), (), s32[]{:S(2)}) async-start(), calls=%async_computation.9 | async-start | bytes 4456448 | tf_op jit(solution)/shard_map/all_gather | solution.py:47
  8.6 252.6 %all-gather.9.cloned.1.call-start = ((), (), s32[]{:S(2)}) async-start(), calls=%async_computation.5 | async-start | bytes 5242880 | tf_op jit(solution)/shard_map/all_gather | solution.py:42
  9.4 304.7 %all-gather.7.cloned.1.call-start = ((), (), s32[]{:S(2)}) async-start(), calls=%async_computation.4 | async-start | bytes 5242880 | tf_op jit(solution)/shard_map/all_gather | solution.py:43
  13.4 204.0 %all-to-all-start = ((bf16[4,2048,256]{2,1,0:T(8,128)(2,1)}), bf16[4,2048,256]{2,1,0:T(8,128)(2,1)}, u32[]{:S(2)}, u32[]{:S(2)}) async-start(bf16[4,2048,256]{2,1,0:T(8,128)(2,1)} %stack.2), calls=%async_computation | async-start | bytes 8388608 | tf_op jit(solution)/shard_map/all_to_all | solution.py:40
  20.5 618.9 %reduce-scatter.4.cloned.1.call-start = ((), (), s32[]{:S(2)}) async-start(), calls=%async_computation.6 | async-start | bytes 5242880 | tf_op jit(solution)/shard_map/reduce_scatter | solution.py:56
  319.5 0.6 copy-start.2
  323.4 318.3 %reduce-scatter.6.cloned.1.call-start = ((), (), s32[]{:S(2)}) async-start(), calls=%async_computation.7 | async-start | bytes 5242880 | tf_op jit(solution)/shard_map/reduce_scatter | solution.py:62
  327.5 1.9 copy-start.1
  327.5 5.2 copy-start.5
  327.5 316.4 %reduce-scatter.8.cloned.1.call-start = ((), (), s32[]{:S(2)}) async-start(), calls=%async_computation.8 | async-start | bytes 5242880 | tf_op jit(solution)/shard_map/reduce_scatter | solution.py:68
  332.7 1.3 copy-start.3
  333.9 4.3 copy-start
  334.0 4.3 copy-start.4
Sparse Core Ops, SparseCore 0:
  10.6 102.9 all-gather.12
  116.2 96.5 all-gather.10
  214.6 46.6 all-gather.8
  262.9 51.1 all-gather.6
  323.5 49.0 reduce-scatter.3
  375.2 49.0 reduce-scatter.5
  427.4 49.0 reduce-scatter.7
